TPU v7x, 256 devices: a whole 4x4x8 slice. The times are simulated.
256 devices in a mesh: energy: 64 (over z, x, core), sector: 4 (over y).
Axes of the slice: x: 4, y: 4, z: 8, core: 2. Of those that a mesh axis runs over, the one named last changes fastest.
Arguments:
- boundary: float32 [128, 2, 1024, 128], P('energy'), may hold values from -6 to 6
- energies: float32 [128], P('energy'), may hold values from 0.5 to 1.5
- levels: int32 [1024], replicated, may hold values from 0 to 31
- pattern: int32 [8, 8, 8], P('sector'), may hold values 0 or 1
- coupling: bfloat16 [8, 64, 128, 128], P('sector', 'energy'), may hold values from -0.125 to 0.125
Outputs:
- edge_state: float32 [4, 128, 2, 1024, 128], P('sector', 'energy')
All inputs are finite; a program needn't handle non-finite values. No bound on the sum of `pattern` on one device may be relied on, other than what follows from the above.
Results may differ from a plain program's by a relative error of at most 0.0003.
Values may be sent and summed in bfloat16 or wider, within the bound.
No kernel may reach another device: no remote copies, remote signals or barrier semaphores. Data moves between devices by JAX's collectives and lax.ppermute only.
A program may use at most 64 MiB of HBM per device.

v0:
```python
import jax
import jax.numpy as jnp
from jax import lax
from jax.sharding import Mesh
from jax.sharding import PartitionSpec as P

STEPS = 4
ENERGY = ("energy_0", "energy_1", "energy_2")


def in_order(tiles, dim):
    tiles = jnp.moveaxis(tiles, 0, dim)
    dims = tiles.shape
    return tiles.reshape(*dims[:dim], dims[dim] * dims[dim + 1], *dims[dim + 2 :])


def gather_in_order(x, axes, order):
    tiles = x[None]
    for k in order:
        tiles = lax.all_gather(tiles, axes[k], axis=0, tiled=True)
    held = [lax.axis_size(axes[k]) for k in reversed(order)]
    tiles = tiles.reshape(*held, *x.shape)
    turned = sorted(range(len(order)), key=lambda place: order[len(order) - 1 - place])
    return tiles.transpose(*turned, *range(len(order), tiles.ndim)).reshape(-1, *x.shape)


def gathered_by_axis(x, axes, order, dim):
    return in_order(gather_in_order(x, axes, order), dim)


def shifted(value, axis, steps):
    count = lax.axis_size(axis)
    leading, last = (max(0, -steps), min(count, count - steps))
    return lax.ppermute(value, axis, [(source, source + steps) for source in range(leading, last)])


def body(boundary, energies, levels, pattern, coupling):
    runs = lax.axis_size("sector")
    index = lax.axis_index("sector")
    sec_dev = coupling.shape[0]
    blocks_side = pattern.shape[1]
    width = coupling.shape[2]
    channels = blocks_side * width
    columns = boundary.shape[3]
    step_len = 1.6 / (sec_dev * STEPS * runs)
    gathered = gathered_by_axis(coupling, ENERGY, (1, 0, 2), 1)
    shaped = gathered.reshape(sec_dev, blocks_side, blocks_side, width, width)
    masked = shaped * pattern.astype(jnp.bfloat16)[:, :, :, None, None]
    thresholds = 0.05 * levels.astype(jnp.float32)

    def advance(state, energy_values):
        count = state.shape[0]
        diag_terms = thresholds[None, :, None] - energy_values[:, None, None]
        field = state[:, 0]
        slope = state[:, 1]
        for inner in range(sec_dev):
            for step in range(STEPS):
                low = field.astype(jnp.bfloat16).reshape(count, blocks_side, width, columns)
                coupled = jnp.einsum(
                    "ijab,ejbc->eiac", masked[inner], low, preferred_element_type=jnp.float32
                )
                coupled = coupled.reshape(count, channels, columns)
                slope = slope + step_len * (diag_terms * field + coupled)
                field = field + step_len * slope
        return jnp.stack([field, slope], axis=1)

    def keepsame(state, energy_values):
        return state

    count = energies.shape[0]

    def tick(tick_index, carry):
        received, result = carry
        slot = tick_index - index
        live = jnp.logical_and(slot >= 0, slot < count)
        where_at = jnp.clip(slot, 0, count - 1)
        own = lax.dynamic_slice_in_dim(boundary, where_at, 1, 0)
        energy_now = lax.dynamic_slice_in_dim(energies, where_at, 1, 0)
        start = jnp.where(index == 0, own, received)
        moved = lax.cond(live, advance, keepsame, start, energy_now)
        current = lax.dynamic_slice_in_dim(result, where_at, 1, 0)
        result = lax.dynamic_update_slice_in_dim(
            result, jnp.where(live, moved, current), where_at, 0
        )
        received = shifted(moved, "sector", 1)
        return (received, result)

    first = jnp.zeros_like(boundary[:1])
    received, result = lax.fori_loop(0, runs + count - 1, tick, (first, jnp.zeros_like(boundary)))
    return result[None]


def solution(mesh):
    split = Mesh(
        mesh.devices.reshape(8, 4, 2, mesh.shape["sector"]),
        ("energy_0", "energy_1", "energy_2", "sector"),
    )
    placed = (
        P(ENERGY, None, None, None),
        P(ENERGY),
        P(),
        P("sector", None, None),
        P("sector", ENERGY, None, None),
    )
    return jax.shard_map(
        body,
        mesh=split,
        in_specs=placed,
        out_specs=P("sector", ENERGY, None, None, None),
        check_vma=False,
    )
```

profile of v0, /device:TPU:24, one launch (start us, length us, event | category | flops | bytes accessed | tf_op | source)
XLA Modules:
  0.0 287.6 jit_solution(7945603454623909311)
XLA Ops:
  6.5 14.3 %all-gather = bf16[8,1,128,128]{3,2,1,0:T(8,128)(2,1)} all-gather(bf16[2,1,128,128]{3,2,1,0:T(8,128)(2,1)} %param.13), channel_id=2, replica_groups=mesh['energy_0'=8,'energy_1'=4,'energy_2'=2,'sector'=4] {'energy_1'}, dimensions={0}, use_global_device_ids=true | all-gather | bytes 327680 | tf_op jit(solution)/shard_map/all_gather | solution.py:20
  20.9 42.4 %all-gather.4.cloned.1.call-done = bf16[32,2,1,128,128]{4,3,2,1,0:T(8,128)(2,1)} async-done(((bf16[4,2,1,128,128]{4,3,2,1,0:T(8,128)(2,1)}), bf16[32,2,1,128,128]{4,3,2,1,0:T(8,128)(2,1)}) %all-gather.4.cloned.1.call-update) | async-done | bytes 2097168 | tf_op jit(solution)/shard_map/all_gather | solution.py:20
  63.4 19.3 %all-gather.6.cloned.1.call-done = bf16[64,2,1,128,128]{4,3,2,1,0:T(8,128)(2,1)} async-done(((bf16[32,2,1,128,128]{4,3,2,1,0:T(8,128)(2,1)}), bf16[64,2,1,128,128]{4,3,2,1,0:T(8,128)(2,1)}) %all-gather.6.cloned.1.call-update) | async-done | bytes 4194320 | tf_op jit(solution)/shard_map/all_gather | solution.py:20
  82.7 2.7 copy.11
  85.4 2.3 copy_multiply_fusion
  87.8 1.5 broadcast_in_dim.16
  89.3 191.5 %while.16 = (s32[]{:T(128)}, f32[1,2,1024,128]{3,2,1,0:T(8,128)S(1)}, f32[2,2,1024,128]{3,2,1,0:T(8,128)}, s32[]{:T(128)}, pred[]{:T(512)}, /*index=5*/f32[2,2,1...) while((s32[]{:T(128)}, ...), condition=%wide.region_3.4_spmd, body=%wide.region_0.3_spmd.sunk | while | flops 2166753280 | bytes 80532288 | solution.py:89
  91.9 2.3 select_dynamic-update-slice_fusion.2
  94.2 23.6 %collective-permute-done = f32[1,2,1024,128]{3,2,1,0:T(8,128)S(1)} collective-permute-done((f32[1,2,1024,128]{3,2,1,0:T(8,128)S(1)}, f32[1,2,1024,128]{3,2,1,0:T(8,128)S(1)}, u32[]{:S(2)}, u32[]{:S(2)}) %collective-permute-start) | collective-permute-done | bytes 1048608 | tf_op jit(solution)/shard_map/while/body/eval_jaxpr/ppermute | solution.py:34
  120.5 2.3 select_dynamic-update-slice_fusion.2
  122.8 22.8 %collective-permute-done = f32[1,2,1024,128]{3,2,1,0:T(8,128)S(1)} collective-permute-done((f32[1,2,1024,128]{3,2,1,0:T(8,128)S(1)}, f32[1,2,1024,128]{3,2,1,0:T(8,128)S(1)}, u32[]{:S(2)}, u32[]{:S(2)}) %collective-permute-start) | collective-permute-done | bytes 1048608 | tf_op jit(solution)/shard_map/while/body/eval_jaxpr/ppermute | solution.py:34
  145.6 1.3 dynamic-slice_select_fusion.2
  148.3 2.3 select_dynamic-update-slice_fusion.2
  150.6 54.1 %collective-permute-done = f32[1,2,1024,128]{3,2,1,0:T(8,128)S(1)} collective-permute-done((f32[1,2,1024,128]{3,2,1,0:T(8,128)S(1)}, f32[1,2,1024,128]{3,2,1,0:T(8,128)S(1)}, u32[]{:S(2)}, u32[]{:S(2)}) %collective-permute-start) | collective-permute-done | bytes 1048608 | tf_op jit(solution)/shard_map/while/body/eval_jaxpr/ppermute | solution.py:34
  204.7 1.3 dynamic-slice_select_fusion.2
  206.0 11.7 %conditional.2 = (f32[1,2,1024,128]{3,2,1,0:T(8,128)S(1)}) conditional(s32[]{:T(128)} %convert_element_type.107, f32[1,2,1024,128]{3,2,1,0:T(8,128)S(1)} %dynamic-slice_select_fusion.2, (f32[1,2,1024,128]{3,2,1,0:T(8,128)S(1)}, f32[2]{0:T(128)S(1)}, s32[]{:T(128)}, f32[1024]{0:T(1024)S(1)}, bf16[2,8,8,128,128]{4,3,2,1,0:T(8,128)(2,1)}) %tuple.51), branch_computations={%region_1.1_spmd, %region_2.2_spmd} | conditional | flops 2166228992 | bytes 70045752 | solution.py:80
  208.1 2.4 fusion.14
  219.0 2.3 select_dynamic-update-slice_fusion.2
  221.3 21.9 %collective-permute-done = f32[1,2,1024,128]{3,2,1,0:T(8,128)S(1)} collective-permute-done((f32[1,2,1024,128]{3,2,1,0:T(8,128)S(1)}, f32[1,2,1024,128]{3,2,1,0:T(8,128)S(1)}, u32[]{:S(2)}, u32[]{:S(2)}) %collective-permute-start) | collective-permute-done | bytes 1048608 | tf_op jit(solution)/shard_map/while/body/eval_jaxpr/ppermute | solution.py:34
  243.2 1.3 dynamic-slice_select_fusion.2
  244.5 11.7 %conditional.2 = (f32[1,2,1024,128]{3,2,1,0:T(8,128)S(1)}) conditional(s32[]{:T(128)} %convert_element_type.107, f32[1,2,1024,128]{3,2,1,0:T(8,128)S(1)} %dynamic-slice_select_fusion.2, (f32[1,2,1024,128]{3,2,1,0:T(8,128)S(1)}, f32[2]{0:T(128)S(1)}, s32[]{:T(128)}, f32[1024]{0:T(1024)S(1)}, bf16[2,8,8,128,128]{4,3,2,1,0:T(8,128)(2,1)}) %tuple.51), branch_computations={%region_1.1_spmd, %region_2.2_spmd} | conditional | flops 2166228992 | bytes 70045752 | solution.py:80
  246.6 2.5 fusion.14
  257.5 2.3 select_dynamic-update-slice_fusion.2
  259.8 21.0 %collective-permute-done = f32[1,2,1024,128]{3,2,1,0:T(8,128)S(1)} collective-permute-done((f32[1,2,1024,128]{3,2,1,0:T(8,128)S(1)}, f32[1,2,1024,128]{3,2,1,0:T(8,128)S(1)}, u32[]{:S(2)}, u32[]{:S(2)}) %collective-permute-start) | collective-permute-done | bytes 1048608 | tf_op jit(solution)/shard_map/while/body/eval_jaxpr/ppermute | solution.py:34
  (57 shorter events, 27.5 us)
Async XLA Ops:
  6.5 56.8 %copy-start.1 = (s32[2,8,8]{2,1,0:T(8,128)S(1)}, s32[2,8,8]{2,1,0:T(8,128)}, u32[]{:S(2)}) copy-start(s32[2,8,8]{2,1,0:T(8,128)} %param.12) | copy-start | bytes 1540
  6.5 56.9 %copy-start.2 = (s32[1024]{0:T(1024)S(1)}, s32[1024]{0:T(1024)}, u32[]{:S(2)}) copy-start(s32[1024]{0:T(1024)} %param.11) | copy-start | bytes 12292
  6.5 56.8 %all-gather.4.cloned.1.call-start = ((), (), s32[]{:S(2)}) async-start(), calls=%async_computation | async-start | bytes 2359296 | tf_op jit(solution)/shard_map/all_gather | solution.py:20
  20.9 61.8 %all-gather.6.cloned.1.call-start = ((), (), s32[]{:S(2)}) async-start(), calls=%async_computation.1 | async-start | bytes 6291456 | tf_op jit(solution)/shard_map/all_gather | solution.py:20
  87.7 1.5 copy-start.3
  90.6 27.2 %collective-permute-start = (f32[1,2,1024,128]{3,2,1,0:T(8,128)S(1)}, f32[1,2,1024,128]{3,2,1,0:T(8,128)S(1)}, u32[]{:S(2)}, u32[]{:S(2)}) collective-permute-start(f32[1,2,1024,128]{3,2,1,0:T(8,128)S(1)} %get-tuple-element.329), channel_id=1, source_target_pairs={{0,1},{1,2},{2,3},{4,5},{5,6},{6,7},{8,9},{9,10},{10,11},{12,13},{... | collective-permute-start | bytes 3145736 | tf_op jit(solution)/shard_map/while/body/eval_jaxpr/ppermute | solution.py:34
  119.2 26.4 %collective-permute-start = (f32[1,2,1024,128]{3,2,1,0:T(8,128)S(1)}, f32[1,2,1024,128]{3,2,1,0:T(8,128)S(1)}, u32[]{:S(2)}, u32[]{:S(2)}) collective-permute-start(f32[1,2,1024,128]{3,2,1,0:T(8,128)S(1)} %get-tuple-element.329), channel_id=1, source_target_pairs={{0,1},{1,2},{2,3},{4,5},{5,6},{6,7},{8,9},{9,10},{10,11},{12,13},{... | collective-permute-start | bytes 3145736 | tf_op jit(solution)/shard_map/while/body/eval_jaxpr/ppermute | solution.py:34
  147.0 57.7 %collective-permute-start = (f32[1,2,1024,128]{3,2,1,0:T(8,128)S(1)}, f32[1,2,1024,128]{3,2,1,0:T(8,128)S(1)}, u32[]{:S(2)}, u32[]{:S(2)}) collective-permute-start(f32[1,2,1024,128]{3,2,1,0:T(8,128)S(1)} %get-tuple-element.329), channel_id=1, source_target_pairs={{0,1},{1,2},{2,3},{4,5},{5,6},{6,7},{8,9},{9,10},{10,11},{12,13},{... | collective-permute-start | bytes 3145736 | tf_op jit(solution)/shard_map/while/body/eval_jaxpr/ppermute | solution.py:34
  208.1 2.8 copy-start
  217.7 25.5 %collective-permute-start = (f32[1,2,1024,128]{3,2,1,0:T(8,128)S(1)}, f32[1,2,1024,128]{3,2,1,0:T(8,128)S(1)}, u32[]{:S(2)}, u32[]{:S(2)}) collective-permute-start(f32[1,2,1024,128]{3,2,1,0:T(8,128)S(1)} %get-tuple-element.329), channel_id=1, source_target_pairs={{0,1},{1,2},{2,3},{4,5},{5,6},{6,7},{8,9},{9,10},{10,11},{12,13},{... | collective-permute-start | bytes 3145736 | tf_op jit(solution)/shard_map/while/body/eval_jaxpr/ppermute | solution.py:34
  246.6 2.8 copy-start
  256.2 24.6 %collective-permute-start = (f32[1,2,1024,128]{3,2,1,0:T(8,128)S(1)}, f32[1,2,1024,128]{3,2,1,0:T(8,128)S(1)}, u32[]{:S(2)}, u32[]{:S(2)}) collective-permute-start(f32[1,2,1024,128]{3,2,1,0:T(8,128)S(1)} %get-tuple-element.329), channel_id=1, source_target_pairs={{0,1},{1,2},{2,3},{4,5},{5,6},{6,7},{8,9},{9,10},{10,11},{12,13},{... | collective-permute-start | bytes 3145736 | tf_op jit(solution)/shard_map/while/body/eval_jaxpr/ppermute | solution.py:34
Sparse Core Ops, SparseCore 0:
  21.0 42.2 all-gather.3
  65.1 17.5 all-gather.5
where the time goes:
time: 288 us
  waiting for transfers between devices  205 us (71%)
  other arithmetic  25.6 us (9%)
  matrix products  15.9 us (6%)
  blocking collectives  14.3 us (5%)
  between operations  13.5 us (5%)
  starting transfers between devices  6.5 us (2%)
  local copies, waits for them, and re-layouts  6.31 us (2%)
    ppermute x5, waiting for transfers between devices, shifted(): lax.ppermute(value, axis, [(source, source + steps) for source in range(l...  143 us
    all_gather x2, waiting for transfers between devices, gather_in_order(): tiles = lax.all_gather(tiles, axes[k], axis=0, tiled=True)  61.7 us
    dot_general x16, matrix products, advance(): jnp.einsum('ijab,ejbc->eiac', masked[inner], low, preferred_element_type=...  15.9 us
    all_gather x1, blocking collectives, gather_in_order(): tiles = lax.all_gather(tiles, axes[k], axis=0, tiled=True)  14.3 us
    dynamic_update_slice x5, other arithmetic, tick(): lax.dynamic_update_slice_in_dim(result, jnp.where(live, moved, current),...  11.5 us
    select_n x5, other arithmetic, tick(): start = jnp.where(index == 0, own, received)  6.64 us
    ppermute x5, starting transfers between devices, shifted(): lax.ppermute(value, axis, [(source, source + steps) for source in range(l...  6.46 us
  transfers between devices with their start and end apart: 7, of which 7 were waited for; matrix products, arithmetic and copies ran while one was open for 4% of the time, Pallas kernels for 0%

commit v1 on v0

--- a/solution.py
+++ b/solution.py
@@ -3,6 +3,7 @@
 from jax import lax
 from jax.sharding import Mesh
 from jax.sharding import PartitionSpec as P
+from jax.lax import all_to_all, axis_size
 
 STEPS = 4
 ENERGY = ("energy_0", "energy_1", "energy_2")
@@ -17,7 +18,16 @@
 def gather_in_order(x, axes, order):
     tiles = x[None]
     for k in order:
-        tiles = lax.all_gather(tiles, axes[k], axis=0, tiled=True)
+        inner_x = axes[k]
+        tiles = jnp.concatenate(
+            all_to_all(
+                jnp.stack(axis_size(inner_x) * [tiles]),
+                axis_name=inner_x,
+                split_axis=0,
+                concat_axis=0,
+            ),
+            0,
+        )
     held = [lax.axis_size(axes[k]) for k in reversed(order)]
     tiles = tiles.reshape(*held, *x.shape)
     turned = sorted(range(len(order)), key=lambda place: order[len(order) - 1 - place])

time: 288 us -> 275 us (0.955)
  between operations: 13.5 us -> 0.07 us
  waiting for transfers between devices: 205 us -> 192 us
  starting transfers between devices: 6.5 us -> 15.1 us
  blocking collectives: 14.3 us -> 17.9 us
    all_gather x2 -> x0, waiting for transfers between devices: 61.7 us -> none  [gather_in_order(): tiles = lax.all_gather(tiles, axes[k], axis=0, tiled=True)]
    all_to_all x0 -> x1, waiting for transfers between devices: none -> 49.8 us  [gather_in_order(): all_to_all(jnp.stack(axis_size(inner_x) * [tiles]), axis_name=inner_x, sp...]
    all_to_all x0 -> x2, blocking collectives: none -> 17.9 us  [gather_in_order(): all_to_all(jnp.stack(axis_size(inner_x) * [tiles]), axis_name=inner_x, sp...]
    all_gather x1 -> x0, blocking collectives: 14.3 us -> none  [gather_in_order(): tiles = lax.all_gather(tiles, axes[k], axis=0, tiled=True)]
    all_to_all x0 -> x1, starting transfers between devices: none -> 8.6 us  [gather_in_order(): all_to_all(jnp.stack(axis_size(inner_x) * [tiles]), axis_name=inner_x, sp...]
    another operation x0 -> x4, local copies, waits for them, and re-layouts: none -> 3.29 us  [gather_in_order(): jnp.stack(axis_size(inner_x) * [tiles])]
  transfers between devices with their start and end apart: 7 -> 6, of which waited for: 7 -> 6; matrix products, arithmetic and copies ran while one was open for 4% -> 4% of each run, Pallas kernels for 0% -> 0%
where the time goes in v1:
time: 275 us
  waiting for transfers between devices  192 us (70%)
  other arithmetic  25.8 us (9%)
  blocking collectives  17.9 us (7%)
  matrix products  16.1 us (6%)
  starting transfers between devices  15.1 us (5%)
  local copies, waits for them, and re-layouts  7.34 us (3%)
    ppermute x5, waiting for transfers between devices, shifted(): lax.ppermute(value, axis, [(source, source + steps) for source in range(l...  142 us
    all_to_all x1, waiting for transfers between devices, gather_in_order(): all_to_all(jnp.stack(axis_size(inner_x) * [tiles]), axis_name=inner_x, sp...  49.8 us
    all_to_all x2, blocking collectives, gather_in_order(): all_to_all(jnp.stack(axis_size(inner_x) * [tiles]), axis_name=inner_x, sp...  17.9 us
    dot_general x16, matrix products, advance(): jnp.einsum('ijab,ejbc->eiac', masked[inner], low, preferred_element_type=...  16.1 us
    dynamic_update_slice x5, other arithmetic, tick(): lax.dynamic_update_slice_in_dim(result, jnp.where(live, moved, current),...  11.5 us
    all_to_all x1, starting transfers between devices, gather_in_order(): all_to_all(jnp.stack(axis_size(inner_x) * [tiles]), axis_name=inner_x, sp...  8.6 us
    select_n x5, other arithmetic, tick(): start = jnp.where(index == 0, own, received)  6.64 us
    ppermute x5, starting transfers between devices, shifted(): lax.ppermute(value, axis, [(source, source + steps) for source in range(l...  6.46 us
  transfers between devices with their start and end apart: 6, of which 6 were waited for; matrix products, arithmetic and copies ran while one was open for 4% of the time, Pallas kernels for 0%

profile of v1, /device:TPU:24, one launch (start us, length us, event | category | flops | bytes accessed | tf_op | source)
XLA Modules:
  0.0 274.6 jit_solution(7546250612630975013)
XLA Ops:
  0.9 10.8 %all_to_all.15 = bf16[4,1,2,1,128,128]{5,4,2,3,1,0:T(8,128)(2,1)S(1)} all-to-all(bf16[4,1,2,1,128,128]{5,4,2,3,1,0:T(8,128)(2,1)S(1)} %stack.14), channel_id=1, replica_groups=mesh['energy_0'=8,'energy_1'=4,'energy_2'=2,'sector'=4] {'energy_1'}, dimensions={0} | all-to-all | bytes 524288 | tf_op jit(solution)/shard_map/all_to_all | solution.py:23
  11.7 1.8 stack.15
  13.5 8.6 %all-to-all-start.1 = ((bf16[8,4,2,1,128,128]{5,4,1,2,3,0:T(8,128)(2,1)}), bf16[8,4,2,1,128,128]{5,4,1,2,3,0:T(8,128)(2,1)S(1)}, u32[]{:S(2)}, u32[]{:S(2)}) async-start(bf16[8,4,2,1,128,128]{5,4,1,2,3,0:T(8,128)(2,1)} %stack.15), calls=%async_computation.1 | async-start | bytes 4194304 | tf_op jit(solution)/shard_map/all_to_all | solution.py:23
  22.1 49.8 %all-to-all-done.1 = bf16[8,4,2,1,128,128]{5,4,1,2,3,0:T(8,128)(2,1)S(1)} async-done(((bf16[8,4,2,1,128,128]{5,4,1,2,3,0:T(8,128)(2,1)}), bf16[8,4,2,1,128,128]{5,4,1,2,3,0:T(8,128)(2,1)S(1)}, u32[]{:S(2)}, u32[]{:S(2)}) %all-to-all-start.1) | async-done | bytes 2097184 | tf_op jit(solution)/shard_map/all_to_all | solution.py:23
  73.0 7.1 %all_to_all.16 = bf16[2,32,2,1,128,128]{5,4,1,2,3,0:T(8,128)(2,1)S(1)} all-to-all(bf16[2,32,2,1,128,128]{5,4,1,2,3,0:T(8,128)(2,1)S(1)} %copy.9), channel_id=1, replica_groups=mesh['energy_0'=8,'energy_1'=4,'energy_2'=2,'sector'=4] {'energy_2'}, dimensions={0} | all-to-all | bytes 8388608 | tf_op jit(solution)/shard_map/all_to_all | solution.py:23
  80.5 2.3 copy_multiply_fusion
  82.8 1.5 broadcast_in_dim.13
  84.3 190.3 %while.16 = (s32[]{:T(128)}, f32[1,2,1024,128]{3,2,1,0:T(8,128)S(1)}, f32[2,2,1024,128]{3,2,1,0:T(8,128)}, s32[]{:T(128)}, pred[]{:T(512)}, /*index=5*/f32[2,2,1...) while((s32[]{:T(128)}, ...), condition=%wide.region_3.4_spmd, body=%wide.region_0.3_spmd.sunk | while | flops 2166753280 | bytes 80532288 | solution.py:99
  84.3 1.3 dynamic-slice_select_fusion.2
  86.9 2.3 select_dynamic-update-slice_fusion.2
  89.2 23.5 %collective-permute-done = f32[1,2,1024,128]{3,2,1,0:T(8,128)S(1)} collective-permute-done((f32[1,2,1024,128]{3,2,1,0:T(8,128)S(1)}, f32[1,2,1024,128]{3,2,1,0:T(8,128)S(1)}, u32[]{:S(2)}, u32[]{:S(2)}) %collective-permute-start) | collective-permute-done | bytes 1048608 | tf_op jit(solution)/shard_map/while/body/eval_jaxpr/ppermute | solution.py:44
  115.4 2.3 select_dynamic-update-slice_fusion.2
  117.7 22.6 %collective-permute-done = f32[1,2,1024,128]{3,2,1,0:T(8,128)S(1)} collective-permute-done((f32[1,2,1024,128]{3,2,1,0:T(8,128)S(1)}, f32[1,2,1024,128]{3,2,1,0:T(8,128)S(1)}, u32[]{:S(2)}, u32[]{:S(2)}) %collective-permute-start) | collective-permute-done | bytes 1048608 | tf_op jit(solution)/shard_map/while/body/eval_jaxpr/ppermute | solution.py:44
  140.3 1.3 dynamic-slice_select_fusion.2
  143.0 2.3 select_dynamic-update-slice_fusion.2
  145.3 53.4 %collective-permute-done = f32[1,2,1024,128]{3,2,1,0:T(8,128)S(1)} collective-permute-done((f32[1,2,1024,128]{3,2,1,0:T(8,128)S(1)}, f32[1,2,1024,128]{3,2,1,0:T(8,128)S(1)}, u32[]{:S(2)}, u32[]{:S(2)}) %collective-permute-start) | collective-permute-done | bytes 1048608 | tf_op jit(solution)/shard_map/while/body/eval_jaxpr/ppermute | solution.py:44
  200.0 11.7 %conditional.2 = (f32[1,2,1024,128]{3,2,1,0:T(8,128)S(1)}) conditional(s32[]{:T(128)} %convert_element_type.107, f32[1,2,1024,128]{3,2,1,0:T(8,128)S(1)} %dynamic-slice_select_fusion.2, (f32[1,2,1024,128]{3,2,1,0:T(8,128)S(1)}, f32[2]{0:T(128)S(1)}, s32[]{:T(128)}, f32[1024]{0:T(1024)S(1)}, bf16[2,8,8,128,128]{4,3,2,1,0:T(8,128)(2,1)}) %tuple.51), branch_computations={%region_1.1_spmd, %region_2.2_spmd} | conditional | flops 2166228992 | bytes 70045752 | solution.py:90
  202.0 2.5 fusion.14
  213.0 2.3 select_dynamic-update-slice_fusion.2
  215.3 21.8 %collective-permute-done = f32[1,2,1024,128]{3,2,1,0:T(8,128)S(1)} collective-permute-done((f32[1,2,1024,128]{3,2,1,0:T(8,128)S(1)}, f32[1,2,1024,128]{3,2,1,0:T(8,128)S(1)}, u32[]{:S(2)}, u32[]{:S(2)}) %collective-permute-start) | collective-permute-done | bytes 1048608 | tf_op jit(solution)/shard_map/while/body/eval_jaxpr/ppermute | solution.py:44
  238.4 11.7 %conditional.2 = (f32[1,2,1024,128]{3,2,1,0:T(8,128)S(1)}) conditional(s32[]{:T(128)} %convert_element_type.107, f32[1,2,1024,128]{3,2,1,0:T(8,128)S(1)} %dynamic-slice_select_fusion.2, (f32[1,2,1024,128]{3,2,1,0:T(8,128)S(1)}, f32[2]{0:T(128)S(1)}, s32[]{:T(128)}, f32[1024]{0:T(1024)S(1)}, bf16[2,8,8,128,128]{4,3,2,1,0:T(8,128)(2,1)}) %tuple.51), branch_computations={%region_1.1_spmd, %region_2.2_spmd} | conditional | flops 2166228992 | bytes 70045752 | solution.py:90
  240.4 2.4 fusion.14
  251.4 2.3 select_dynamic-update-slice_fusion.2
  253.7 20.9 %collective-permute-done = f32[1,2,1024,128]{3,2,1,0:T(8,128)S(1)} collective-permute-done((f32[1,2,1024,128]{3,2,1,0:T(8,128)S(1)}, f32[1,2,1024,128]{3,2,1,0:T(8,128)S(1)}, u32[]{:S(2)}, u32[]{:S(2)}) %collective-permute-start) | collective-permute-done | bytes 1048608 | tf_op jit(solution)/shard_map/while/body/eval_jaxpr/ppermute | solution.py:44
  (60 shorter events, 31.1 us)
Async XLA Ops:
  13.5 8.6 %copy-start.1 = (s32[2,8,8]{2,1,0:T(8,128)S(1)}, s32[2,8,8]{2,1,0:T(8,128)}, u32[]{:S(2)}) copy-start(s32[2,8,8]{2,1,0:T(8,128)} %param.12) | copy-start | bytes 1540
  13.5 8.6 %copy-start.2 = (s32[1024]{0:T(1024)S(1)}, s32[1024]{0:T(1024)}, u32[]{:S(2)}) copy-start(s32[1024]{0:T(1024)} %param.11) | copy-start | bytes 12292
  13.5 58.4 %all-to-all-start.1 = ((bf16[8,4,2,1,128,128]{5,4,1,2,3,0:T(8,128)(2,1)}), bf16[8,4,2,1,128,128]{5,4,1,2,3,0:T(8,128)(2,1)S(1)}, u32[]{:S(2)}, u32[]{:S(2)}) async-start(bf16[8,4,2,1,128,128]{5,4,1,2,3,0:T(8,128)(2,1)} %stack.15), calls=%async_computation.1 | async-start | bytes 4194304 | tf_op jit(solution)/shard_map/all_to_all | solution.py:23
  82.7 1.5 copy-start.3
  85.6 27.1 %collective-permute-start = (f32[1,2,1024,128]{3,2,1,0:T(8,128)S(1)}, f32[1,2,1024,128]{3,2,1,0:T(8,128)S(1)}, u32[]{:S(2)}, u32[]{:S(2)}) collective-permute-start(f32[1,2,1024,128]{3,2,1,0:T(8,128)S(1)} %get-tuple-element.329), channel_id=1, source_target_pairs={{0,1},{1,2},{2,3},{4,5},{5,6},{6,7},{8,9},{9,10},{10,11},{12,13},{... | collective-permute-start | bytes 3145736 | tf_op jit(solution)/shard_map/while/body/eval_jaxpr/ppermute | solution.py:44
  114.1 26.2 %collective-permute-start = (f32[1,2,1024,128]{3,2,1,0:T(8,128)S(1)}, f32[1,2,1024,128]{3,2,1,0:T(8,128)S(1)}, u32[]{:S(2)}, u32[]{:S(2)}) collective-permute-start(f32[1,2,1024,128]{3,2,1,0:T(8,128)S(1)} %get-tuple-element.329), channel_id=1, source_target_pairs={{0,1},{1,2},{2,3},{4,5},{5,6},{6,7},{8,9},{9,10},{10,11},{12,13},{... | collective-permute-start | bytes 3145736 | tf_op jit(solution)/shard_map/while/body/eval_jaxpr/ppermute | solution.py:44
  141.7 57.0 %collective-permute-start = (f32[1,2,1024,128]{3,2,1,0:T(8,128)S(1)}, f32[1,2,1024,128]{3,2,1,0:T(8,128)S(1)}, u32[]{:S(2)}, u32[]{:S(2)}) collective-permute-start(f32[1,2,1024,128]{3,2,1,0:T(8,128)S(1)} %get-tuple-element.329), channel_id=1, source_target_pairs={{0,1},{1,2},{2,3},{4,5},{5,6},{6,7},{8,9},{9,10},{10,11},{12,13},{... | collective-permute-start | bytes 3145736 | tf_op jit(solution)/shard_map/while/body/eval_jaxpr/ppermute | solution.py:44
  202.0 2.8 %copy-start = (bf16[2,8,8,128,128]{4,3,2,1,0:T(8,128)(2,1)S(1)}, bf16[2,8,8,128,128]{4,3,2,1,0:T(8,128)(2,1)}, u32[]{:S(2)}) copy-start(bf16[2,8,8,128,128]{4,3,2,1,0:T(8,128)(2,1)} %get-tuple-element.194) | copy-start | bytes 12582916 | tf_op jit(solution)/shard_map/while/body/eval_jaxpr/cond
  211.7 25.4 %collective-permute-start = (f32[1,2,1024,128]{3,2,1,0:T(8,128)S(1)}, f32[1,2,1024,128]{3,2,1,0:T(8,128)S(1)}, u32[]{:S(2)}, u32[]{:S(2)}) collective-permute-start(f32[1,2,1024,128]{3,2,1,0:T(8,128)S(1)} %get-tuple-element.329), channel_id=1, source_target_pairs={{0,1},{1,2},{2,3},{4,5},{5,6},{6,7},{8,9},{9,10},{10,11},{12,13},{... | collective-permute-start | bytes 3145736 | tf_op jit(solution)/shard_map/while/body/eval_jaxpr/ppermute | solution.py:44
  240.4 2.8 %copy-start = (bf16[2,8,8,128,128]{4,3,2,1,0:T(8,128)(2,1)S(1)}, bf16[2,8,8,128,128]{4,3,2,1,0:T(8,128)(2,1)}, u32[]{:S(2)}) copy-start(bf16[2,8,8,128,128]{4,3,2,1,0:T(8,128)(2,1)} %get-tuple-element.194) | copy-start | bytes 12582916 | tf_op jit(solution)/shard_map/while/body/eval_jaxpr/cond
  250.1 24.5 %collective-permute-start = (f32[1,2,1024,128]{3,2,1,0:T(8,128)S(1)}, f32[1,2,1024,128]{3,2,1,0:T(8,128)S(1)}, u32[]{:S(2)}, u32[]{:S(2)}) collective-permute-start(f32[1,2,1024,128]{3,2,1,0:T(8,128)S(1)} %get-tuple-element.329), channel_id=1, source_target_pairs={{0,1},{1,2},{2,3},{4,5},{5,6},{6,7},{8,9},{9,10},{10,11},{12,13},{... | collective-permute-start | bytes 3145736 | tf_op jit(solution)/shard_map/while/body/eval_jaxpr/ppermute | solution.py:44
